TPU v7x, 256 devices: a whole 4x4x8 slice. The times are simulated.
256 devices in a mesh: chan: 8 (over z_lo, core), region: 32 (over x, y, z_hi).
Axes of the slice: x: 4, y: 4, z: 8 (z_hi: 2, z_lo: 4; z = z_hi * 4 + z_lo), core: 2. Of those that a mesh axis runs over, the one named last changes fastest.
Arguments:
- latent: bfloat16 [32, 24, 24, 12, 128], P('region'), may hold values from -6 to 6
- cond_scale: float32 [128], replicated, may hold values from 0.5 to 1.5
- cond_shift: float32 [128], replicated, may hold values from -3 to 3
- fine_weight: bfloat16 [3, 3, 3, 128, 128], replicated, may hold values from -0.109375 to 0.109375
- fine_bias: float32 [128], replicated, may hold values from -3 to 3
- proj_weight: bfloat16 [8192, 1024], P(('chan', 'region')), may hold values from -0.0625 to 0.0625
- proj_bias: float32 [1024], replicated, may hold values from -3 to 3
- bottle_weight: bfloat16 [27, 1024, 1024], P(None, 'chan'), may hold values from -0.0390625 to 0.0390625
- bottle_bias: float32 [1024], replicated, may hold values from -3 to 3
- guide: float32 [1], replicated, may hold values from 1.5 to 4
Outputs:
- guided: bfloat16 [32, 6, 6, 3, 1024], P('region', None, None, None, 'chan')
All inputs are finite; a program needn't handle non-finite values.
Results may differ from a plain program's by a relative error of at most 0.012.
The roundings to bfloat16 on the way count: a program that leaves them out, or rounds other values in their place, can miss the bound.
Values may be sent and summed in bfloat16 or wider, within the bound.
A program may use at most 128 MiB of HBM per device.

v0:
```python
import jax
import jax.numpy as jnp
from jax import lax
from jax.sharding import PartitionSpec as P

FINE_WIDTH = 128
COARSE_WIDTH = 1024
TILE_SIDE = 12
STRIDE = 4
REGIONS_Y = 4
REGIONS_Z = 2


def passed_along(value, axis, steps):
    count = lax.axis_size(axis)
    leading, last = (max(0, -steps), min(count, count - steps))
    return lax.ppermute(value, axis, [(source, source + steps) for source in range(leading, last)])


def extend(block, axis_dim, stride, count):
    place = lax.axis_index("region") // stride % count
    length = block.shape[axis_dim]
    last_layer = lax.slice_in_dim(block, length - 1, length, axis=axis_dim)
    first_layer = lax.slice_in_dim(block, 0, 1, axis=axis_dim)
    arrived = [
        passed_along(layer, "region", offset)
        for layer, offset in ((last_layer, stride), (first_layer, -stride))
    ]
    below = jnp.where(place > 0, arrived[0], jnp.zeros_like(arrived[0]))
    above = jnp.where(place < count - 1, arrived[1], jnp.zeros_like(arrived[1]))
    return jnp.concatenate([below, block, above], axis=axis_dim)


def surround(block, lead):
    count_x = lax.axis_size("region") // (REGIONS_Y * REGIONS_Z)
    block = extend(block, lead + 2, 1, REGIONS_Z)
    block = extend(block, lead + 1, REGIONS_Z, REGIONS_Y)
    return extend(block, lead, REGIONS_Y * REGIONS_Z, count_x)


def fine_conv(window, weight, bias, side):
    stacked = jnp.concatenate(
        [
            window[step_x : step_x + side, step_y : step_y + side, step_z : step_z + side]
            for step_x in range(3)
            for step_y in range(3)
            for step_z in range(3)
        ],
        axis=3,
    )
    stacked = stacked.reshape(side**3, -1)
    total = jnp.dot(
        stacked, weight.reshape(-1, weight.shape[4]), preferred_element_type=jnp.float32
    )
    return jax.nn.silu(total + bias).astype(jnp.bfloat16).reshape(side, side, side, -1)


def to_patches(tile, side):
    cells = side // STRIDE
    grid = tile.reshape(cells, STRIDE, cells, STRIDE, cells, STRIDE, tile.shape[3])
    grid = grid.transpose(0, 2, 4, 6, 1, 3, 5)
    return grid.reshape(cells**3, tile.shape[3] * STRIDE**3)


def shards(
    latent,
    cond_scale,
    cond_shift,
    fine_weight,
    fine_bias,
    proj_weight,
    proj_bias,
    bottle_weight,
    bottle_bias,
    guide,
):
    side = TILE_SIDE
    cells = side // STRIDE
    channels = lax.axis_size("chan")
    chan_place = lax.axis_index("chan")
    per_copy = channels // 2
    tiles_dev = 8 // channels
    copy_index = chan_place // per_copy
    first_tile = chan_place % per_copy * tiles_dev
    width = COARSE_WIDTH // channels
    depth = FINE_WIDTH * STRIDE**3
    block = latent[0].astype(jnp.float32)
    shaped = block * cond_scale + cond_shift
    source = jnp.where(copy_index == 1, shaped, block).astype(jnp.bfloat16)
    padded = surround(source, 0)
    patches = []
    which = first_tile + 0
    window = lax.dynamic_slice(
        padded,
        (which // 2 * side, which % 2 * side, 0, 0),
        (side + 2, side + 2, side + 2, FINE_WIDTH),
    )
    patches.append(to_patches(fine_conv(window, fine_weight, fine_bias, side), side))
    patches = jnp.stack(patches)
    flat = patches.reshape(tiles_dev * cells**3, depth)
    summed = jnp.dot(
        flat,
        lax.all_gather(proj_weight, ("chan", "region"), axis=0, tiled=True),
        preferred_element_type=jnp.float32,
    )
    projected = (summed + proj_bias).astype(jnp.bfloat16)
    coarse = lax.all_to_all(projected, "chan", split_axis=1, concat_axis=0, tiled=True)
    grid = coarse.reshape(2, 2, 2, cells, cells, cells, width).transpose(0, 1, 3, 2, 4, 5, 6)
    grid = grid.reshape(2, 2 * cells, 2 * cells, cells, width)
    framed = surround(grid, 1)
    stacked = jnp.concatenate(
        [
            framed[
                :, step_x : step_x + 2 * cells, step_y : step_y + 2 * cells, step_z : step_z + cells
            ]
            for step_x in range(3)
            for step_y in range(3)
            for step_z in range(3)
        ],
        axis=4,
    )
    stacked = stacked.reshape(-1, 27 * width)
    terms = jnp.dot(
        stacked, bottle_weight.reshape(27 * width, COARSE_WIDTH), preferred_element_type=jnp.float32
    )
    summed = lax.psum_scatter(terms, "chan", scatter_dimension=1, tiled=True)
    bottle = jax.nn.silu(summed + lax.dynamic_slice_in_dim(bottle_bias, chan_place * width, width))
    bottle = bottle.reshape(2, 2 * cells, 2 * cells, cells, width)
    guided = (bottle[0] + guide[0] * (bottle[1] - bottle[0])).astype(jnp.bfloat16)
    return guided[None]


def solution(mesh):
    placed = (
        P("region", None, None, None, None),
        P(),
        P(),
        P(),
        P(),
        P(("chan", "region"), None),
        P(),
        P(None, "chan", None),
        P(),
        P(),
    )
    return jax.shard_map(
        shards,
        mesh=mesh,
        in_specs=placed,
        out_specs=P("region", None, None, None, "chan"),
        check_vma=False,
    )
```

profile of v0, /device:TPU:2, one launch (start us, length us, event | category | flops | bytes accessed | tf_op | source)
XLA Modules:
  0.0 859.1 jit_solution(12610991419264779117)
XLA Ops:
  6.5 0.7 all-gather.2.cloned.1.call-update
  7.3 2.1 fusion.1
  9.4 9.1 %collective-permute-start = (bf16[24,24,1,128]{3,1,2,0:T(8,128)(2,1)S(1)}, bf16[24,24,1,128]{3,1,2,0:T(8,128)(2,1)S(1)}, u32[]{:S(2)}, u32[]{:S(2)}) collective-permute-start(bf16[24,24,1,128]{3,1,2,0:T(8,128)(2,1)S(1)} %get-tuple-element.9), channel_id=1, source_target_pairs={{0,1},{1,2},{2,3},{3,4},{4,5},{5,6},{6,7},{7,8},{8,9},{9,10},{10,1... | collective-permute-start | bytes 442376 | tf_op jit(solution)/shard_map/ppermute | solution.py:17
  18.5 4.3 collective-permute-start.1
  22.9 2.0 collective-permute-done
  24.9 10.2 %collective-permute-done.1 = bf16[24,24,1,128]{3,1,2,0:T(8,128)(2,1)S(1)} collective-permute-done((bf16[24,24,1,128]{3,1,2,0:T(8,128)(2,1)S(1)}, bf16[24,24,1,128]{3,1,2,0:T(8,128)(2,1)S(1)}, u32[]{:S(2)}, u32[]{:S(2)}) %collective-permute-start.1) | collective-permute-done | bytes 147488 | tf_op jit(solution)/shard_map/ppermute | solution.py:17
  35.1 0.3 pad_maximum_fusion.2
  35.4 3.4 collective-permute-start.2
  38.8 4.6 collective-permute-start.3
  43.4 2.0 collective-permute-done.2
  45.6 0.8 collective-permute-done.3
  46.7 0.8 pad_maximum_fusion.4
  47.4 2.9 collective-permute-start.5
  50.4 3.1 collective-permute-start.4
  53.5 0.9 collective-permute-done.5
  54.4 2.7 collective-permute-done.4
  57.2 1.9 fusion.4
  59.2 0.2 slice_dynamic-update-slice_fusion.25
  59.4 0.2 slice_dynamic-update-slice_fusion.24
  59.7 0.3 slice_dynamic-update-slice_fusion.23
  60.0 0.3 slice_dynamic-update-slice_fusion.22
  60.3 0.3 slice_dynamic-update-slice_fusion.21
  60.7 0.3 slice_dynamic-update-slice_fusion.20
  61.0 0.3 slice_dynamic-update-slice_fusion.19
  61.3 0.3 slice_dynamic-update-slice_fusion.18
  61.7 0.2 slice_dynamic-update-slice_fusion.17
  62.4 0.3 slice_dynamic-update-slice_fusion.14
  62.8 0.3 slice_dynamic-update-slice_fusion.13
  63.1 0.3 slice_dynamic-update-slice_fusion.12
  63.4 0.3 slice_dynamic-update-slice_fusion.11
  63.7 0.3 slice_dynamic-update-slice_fusion.10
  64.1 0.3 slice_dynamic-update-slice_fusion.9
  64.7 0.2 slice_dynamic-update-slice_fusion.7
  65.2 0.3 slice_dynamic-update-slice_fusion.5
  65.5 0.3 slice_dynamic-update-slice_fusion.4
  65.8 0.3 slice_dynamic-update-slice_fusion.3
  66.1 0.3 slice_dynamic-update-slice_fusion.2
  66.5 0.3 slice_dynamic-update-slice_fusion.1
  66.8 0.3 slice_dynamic-update-slice_fusion
  67.1 9.4 %copy.70 = bf16[12,12,12,3456]{3,2,1,0:T(8,128)(2,1)} copy(bf16[12,12,12,3456]{3,1,2,0:T(8,128)(2,1)S(1)} %slice_dynamic-update-slice_fusion) | data formatting | bytes 23887872 | tf_op jit(solution)/shard_map/concatenate | solution.py:42
  76.5 18.7 %reshape.92 = bf16[1728,3456]{1,0:T(8,128)(2,1)} reshape(bf16[12,12,12,3456]{3,2,1,0:T(8,128)(2,1)} %copy.70) | data formatting | bytes 23887872 | tf_op jit(solution)/shard_map/reshape | solution.py:51
  95.2 7.7 multiply_convert_fusion
  102.9 17.5 %copy.71 = bf16[3,4,3,4,3,4,128]{5,3,1,6,4,2,0:T(4,128)(2,1)} copy(bf16[3,4,3,4,3,4,128]{6,5,4,3,2,1,0:T(4,128)(2,1)S(1)} %bitcast.33) | data formatting | bytes 884736 | tf_op jit(solution)/shard_map/reshape;reshape | solution.py:60
  120.4 37.1 %reshape_stack_reshape.3 = bf16[27,8192]{1,0:T(8,128)(2,1)S(1)} reshape(bf16[3,3,3,128,4,4,4]{6,5,4,3,2,1,0:T(4,128)(2,1)} %bitcast.24) | data formatting | bytes 884736 | tf_op jit(solution)/shard_map/reshape;stack;reshape | solution.py:100
  157.5 585.9 %all-gather.2.cloned.1.call-done = bf16[8192,1024]{1,0:T(8,128)(2,1)} async-done(((bf16[32,1024]{1,0:T(8,128)(2,1)}), bf16[8192,1024]{1,0:T(8,128)(2,1)}) %all-gather.2.cloned.1.call-update) | async-done | bytes 16777232 | tf_op jit(solution)/shard_map/all_gather | solution.py:103
  743.4 8.8 %fusion.2 = bf16[27,1024]{1,0:T(8,128)(2,1)S(1)} fusion(bf16[27,8192]{1,0:T(8,128)(2,1)S(1)} %reshape_stack_reshape.3, bf16[8192,1024]{1,0:T(8,128)(2,1)} %all-gather.2.cloned.1.call-done, f32[1024]{0:T(1024)S(1)} %copy-done.2), kind=kOutput, calls=%fused_computation.13 | convolution fusion | flops 453040128 | bytes 17278976 | tf_op jit(solution)/shard_map/dot_general | solution.py:101
  752.2 19.5 %all_to_all.16 = bf16[27,8,128]{2,0,1:T(8,128)(2,1)S(1)} all-to-all(bf16[27,8,128]{2,0,1:T(8,128)(2,1)S(1)} %copy.72), channel_id=1, replica_groups=mesh['chan'=8,'region'=32] {'chan'}, dimensions={1} | all-to-all | bytes 110592 | tf_op jit(solution)/shard_map/all_to_all | solution.py:107
  771.8 3.2 collective-permute-start.6
  775.1 9.8 %collective-permute-start.7 = (bf16[2,6,6,1,128]{4,0,3,2,1:T(2,128)(2,1)S(1)}, bf16[2,6,6,1,128]{4,0,3,2,1:T(2,128)(2,1)S(1)}, u32[]{:S(2)}, u32[]{:S(2)}) collective-permute-start(bf16[2,6,6,1,128]{4,0,3,2,1:T(2,128)(2,1)S(1)} %get-tuple-element.48), channel_id=1, source_target_pairs={{1,0},{2,1},{3,2},{4,3},{5,4},{6,5},{7,6},{8,7},{9,8},{10,9},{11,1... | collective-permute-start | bytes 55304 | tf_op jit(solution)/shard_map/ppermute | solution.py:17
  785.0 1.4 collective-permute-done.7
  786.4 1.9 collective-permute-start.8
  788.6 6.0 collective-permute-start.9
  794.8 1.3 collective-permute-done.9
  796.1 0.3 pad_maximum_fusion.9
  796.5 1.9 collective-permute-start.10
  798.7 3.9 collective-permute-start.11
  803.1 1.3 collective-permute-done.11
  804.4 0.5 pad_maximum_fusion.3
  804.9 0.6 fusion.10
  807.6 5.8 fusion.16
  814.1 0.8 dynamic_slice.7
  814.8 35.8 %reduce-scatter.2.cloned.1.call-done = f32[216,128]{1,0:T(8,128)} async-done(((f32[216,1024]{1,0:T(8,128)}), f32[216,128]{1,0:T(8,128)}) %reduce-scatter.2.cloned.1.call-update) | async-done | bytes 110608 | tf_op jit(solution)/shard_map/reduce_scatter | solution.py:126
  850.6 0.9 divide_multiply_fusion
  851.6 0.6 add_convert_fusion
  (126 shorter events, 4.8 us)
Async XLA Ops:
  6.5 88.6 %copy-start = (bf16[3,3,3,128,128]{4,3,2,1,0:T(8,128)(2,1)S(1)}, bf16[3,3,3,128,128]{4,3,2,1,0:T(8,128)(2,1)}, u32[]{:S(2)}) copy-start(bf16[3,3,3,128,128]{4,3,2,1,0:T(8,128)(2,1)} %param.13) | copy-start | bytes 2654212
  6.5 736.9 %all-gather.2.cloned.1.call-start = ((), (), s32[]{:S(2)}) async-start(), calls=%async_computation.2 | async-start | bytes 16842752 | tf_op jit(solution)/shard_map/all_gather | solution.py:103
  7.3 843.3 %reduce-scatter.2.cloned.1.call-start = ((), (), s32[]{:S(2)}) async-start(), calls=%async_computation.3 | async-start | bytes 995328 | tf_op jit(solution)/shard_map/reduce_scatter | solution.py:126
  9.4 15.5 %collective-permute-start = (bf16[24,24,1,128]{3,1,2,0:T(8,128)(2,1)S(1)}, bf16[24,24,1,128]{3,1,2,0:T(8,128)(2,1)S(1)}, u32[]{:S(2)}, u32[]{:S(2)}) collective-permute-start(bf16[24,24,1,128]{3,1,2,0:T(8,128)(2,1)S(1)} %get-tuple-element.9), channel_id=1, source_target_pairs={{0,1},{1,2},{2,3},{3,4},{4,5},{5,6},{6,7},{7,8},{8,9},{9,10},{10,1... | collective-permute-start | bytes 442376 | tf_op jit(solution)/shard_map/ppermute | solution.py:17
  18.5 16.5 %collective-permute-start.1 = (bf16[24,24,1,128]{3,1,2,0:T(8,128)(2,1)S(1)}, bf16[24,24,1,128]{3,1,2,0:T(8,128)(2,1)S(1)}, u32[]{:S(2)}, u32[]{:S(2)}) collective-permute-start(bf16[24,24,1,128]{3,1,2,0:T(8,128)(2,1)S(1)} %get-tuple-element.10), channel_id=1, source_target_pairs={{1,0},{2,1},{3,2},{4,3},{5,4},{6,5},{7,6},{8,7},{9,8},{10,9},{11,1... | collective-permute-start | bytes 442376 | tf_op jit(solution)/shard_map/ppermute | solution.py:17
  35.4 10.0 %collective-permute-start.2 = (bf16[24,1,14,128]{3,1,2,0:T(2,128)(2,1)S(1)}, bf16[24,1,14,128]{3,1,2,0:T(2,128)(2,1)S(1)}, u32[]{:S(2)}, u32[]{:S(2)}) collective-permute-start(bf16[24,1,14,128]{3,1,2,0:T(2,128)(2,1)S(1)} %get-tuple-element.7), channel_id=1, source_target_pairs={{0,2},{1,3},{2,4},{3,5},{4,6},{5,7},{6,8},{7,9},{8,10},{9,11},{10,... | collective-permute-start | bytes 258056 | tf_op jit(solution)/shard_map/ppermute | solution.py:17
  38.8 7.7 collective-permute-start.3
  47.4 7.0 collective-permute-start.5
  50.4 6.8 collective-permute-start.4
  76.5 18.7 %copy-start.3 = (f32[128]{0:T(128)S(1)}, f32[128]{0:T(128)}, u32[]{:S(2)}) copy-start(f32[128]{0:T(128)} %param.14) | copy-start | bytes 1540
  120.4 623.0 %copy-start.2 = (f32[1024]{0:T(1024)S(1)}, f32[1024]{0:T(1024)}, u32[]{:S(2)}) copy-start(f32[1024]{0:T(1024)} %param.16) | copy-start | bytes 12292
  771.8 13.1 %collective-permute-start.6 = (bf16[2,6,6,1,128]{4,0,3,2,1:T(2,128)(2,1)S(1)}, bf16[2,6,6,1,128]{4,0,3,2,1:T(2,128)(2,1)S(1)}, u32[]{:S(2)}, u32[]{:S(2)}) collective-permute-start(bf16[2,6,6,1,128]{4,0,3,2,1:T(2,128)(2,1)S(1)} %get-tuple-element.47), channel_id=1, source_target_pairs={{0,1},{1,2},{2,3},{3,4},{4,5},{5,6},{6,7},{7,8},{8,9},{9,10},{10,1... | collective-permute-start | bytes 55304 | tf_op jit(solution)/shard_map/ppermute | solution.py:17
  775.1 11.2 %collective-permute-start.7 = (bf16[2,6,6,1,128]{4,0,3,2,1:T(2,128)(2,1)S(1)}, bf16[2,6,6,1,128]{4,0,3,2,1:T(2,128)(2,1)S(1)}, u32[]{:S(2)}, u32[]{:S(2)}) collective-permute-start(bf16[2,6,6,1,128]{4,0,3,2,1:T(2,128)(2,1)S(1)} %get-tuple-element.48), channel_id=1, source_target_pairs={{1,0},{2,1},{3,2},{4,3},{5,4},{6,5},{7,6},{8,7},{9,8},{10,9},{11,1... | collective-permute-start | bytes 55304 | tf_op jit(solution)/shard_map/ppermute | solution.py:17
  786.4 8.3 collective-permute-start.8
  788.6 7.5 collective-permute-start.9
  796.5 6.6 collective-permute-start.10
  798.7 5.7 collective-permute-start.11
  807.6 44.7 %copy-start.1 = (bf16[3,3,3,128,128]{4,3,2,1,0:T(8,128)(2,1)S(1)}, bf16[3,3,3,128,128]{4,3,2,1,0:T(8,128)(2,1)}, u32[]{:S(2)}) copy-start(bf16[3,3,3,128,128]{4,3,2,1,0:T(8,128)(2,1)} %param.13) | copy-start | bytes 2654212
Sparse Core Ops, SparseCore 0:
  9.2 734.1 all-gather.1
  813.5 37.0 reduce-scatter.1
where the time goes:
time: 860 us; the launch traced here: 859 us
  waiting for transfers between devices  645 us (75%)
  local copies, waits for them, and re-layouts  94.7 us (11%)
  starting transfers between devices  54.3 us (6%)
  matrix products  22.3 us (3%)
  blocking collectives  19.5 us (2%)
  between operations  15.2 us (2%)
    all_gather x1, waiting for transfers between devices, shards(): lax.all_gather(proj_weight, ('chan', 'region'), axis=0, tiled=True)  586 us
    ppermute x12, starting transfers between devices, passed_along(): lax.ppermute(value, axis, [(source, source + steps) for source in range(l...  54.2 us
    another operation x1, local copies, waits for them, and re-layouts, shards(): flat = patches.reshape(tiles_dev * cells ** 3, depth)  37.1 us
    reduce_scatter x1, waiting for transfers between devices, shards(): summed = lax.psum_scatter(terms, 'chan', scatter_dimension=1, tiled=True)  35.8 us
    ppermute x12, waiting for transfers between devices, passed_along(): lax.ppermute(value, axis, [(source, source + steps) for source in range(l...  22.6 us
    all_to_all x1, blocking collectives, shards(): lax.all_to_all(projected, 'chan', split_axis=1, concat_axis=0, tiled=True)  19.5 us
    reshape x1, local copies, waits for them, and re-layouts, fine_conv(): stacked = stacked.reshape(side ** 3, -1)  18.7 us
    another operation x1, local copies, waits for them, and re-layouts, to_patches(): tile.reshape(cells, STRIDE, cells, STRIDE, cells, STRIDE, tile.shape[3])  17.5 us
  transfers between devices with their start and end apart: 14, of which 11 were waited for; matrix products, arithmetic and copies ran while one was open for 12% of the time, Pallas kernels for 0%

commit v1 on v0

--- a/solution.py
+++ b/solution.py
@@ -100,7 +100,15 @@
     flat = patches.reshape(tiles_dev * cells**3, depth)
     summed = jnp.dot(
         flat,
-        lax.all_gather(proj_weight, ("chan", "region"), axis=0, tiled=True),
+        jnp.concatenate(
+            lax.all_to_all(
+                jnp.stack([proj_weight] * lax.axis_size(("chan", "region"))),
+                ("chan", "region"),
+                0,
+                0,
+            ),
+            axis=0,
+        ),
         preferred_element_type=jnp.float32,
     )
     projected = (summed + proj_bias).astype(jnp.bfloat16)

time: 860 us -> 651 us (0.76)
  waiting for transfers between devices: 645 us -> 410 us
  local copies, waits for them, and re-layouts: 94.7 us -> 112 us
  starting transfers between devices: 54.3 us -> 69.4 us
  blocking collectives: 19.5 us -> 9.04 us
    all_gather x1 -> x0, waiting for transfers between devices: 586 us -> none  [shards(): lax.all_gather(proj_weight, ('chan', 'region'), axis=0, tiled=True)]
    ppermute x12, waiting for transfers between devices: 22.6 us -> 373 us  [passed_along(): lax.ppermute(value, axis, [(source, source + steps) for source in range(l...]
    all_to_all x0 -> x1, starting transfers between devices: none -> 15.7 us  [shards(): lax.all_to_all(jnp.stack([proj_weight] * lax.axis_size(('chan', 'region')...]
    concatenate x2, local copies, waits for them, and re-layouts: 9.68 us -> 20.8 us  [fine_conv(): jnp.concatenate([window[step_x:step_x + side, step_y:step_y + side, step_...]
    all_to_all x1, blocking collectives: 19.5 us -> 9.04 us  [shards(): lax.all_to_all(projected, 'chan', split_axis=1, concat_axis=0, tiled=True)]
  transfers between devices with their start and end apart: 14 -> 14, of which waited for: 11 -> 10; matrix products, arithmetic and copies ran while one was open for 12% -> 18% of each run, Pallas kernels for 0% -> 0%
where the time goes in v1:
time: 651 us; the launch traced here: 646 us
  waiting for transfers between devices  410 us (63%)
  local copies, waits for them, and re-layouts  112 us (17%)
  starting transfers between devices  69.4 us (11%)
  matrix products  22.2 us (3%)
  between operations  15.5 us (2%)
  blocking collectives  9.04 us (1%)
  other arithmetic  8.17 us (1%)
    ppermute x12, waiting for transfers between devices, passed_along(): lax.ppermute(value, axis, [(source, source + steps) for source in range(l...  373 us
    ppermute x12, starting transfers between devices, passed_along(): lax.ppermute(value, axis, [(source, source + steps) for source in range(l...  53.6 us
    another operation x1, local copies, waits for them, and re-layouts, shards(): flat = patches.reshape(tiles_dev * cells ** 3, depth)  37.1 us
    reduce_scatter x1, waiting for transfers between devices, shards(): summed = lax.psum_scatter(terms, 'chan', scatter_dimension=1, tiled=True)  36.9 us
    concatenate x2, local copies, waits for them, and re-layouts, fine_conv(): jnp.concatenate([window[step_x:step_x + side, step_y:step_y + side, step_...  20.8 us
    reshape x1, local copies, waits for them, and re-layouts, fine_conv(): stacked = stacked.reshape(side ** 3, -1)  18.6 us
    another operation x1, local copies, waits for them, and re-layouts, to_patches(): tile.reshape(cells, STRIDE, cells, STRIDE, cells, STRIDE, tile.shape[3])  17.3 us
    all_to_all x1, starting transfers between devices, shards(): lax.all_to_all(jnp.stack([proj_weight] * lax.axis_size(('chan', 'region')...  15.7 us
  transfers between devices with their start and end apart: 14, of which 10 were waited for; matrix products, arithmetic and copies ran while one was open for 18% of the time, Pallas kernels for 0%

profile of v1, /device:TPU:2, one launch (start us, length us, event | category | flops | bytes accessed | tf_op | source)
XLA Modules:
  0.0 646.2 jit_solution(1695571141242845785)
XLA Ops:
  6.5 6.7 %stack.2 = bf16[256,32,1024]{2,1,0:T(8,128)(2,1)} broadcast(bf16[32,1024]{1,0:T(8,128)(2,1)} %param.15), dimensions={1,2} | broadcast | bytes 16842752 | tf_op jit(solution)/shard_map/stack | solution.py:105
  13.3 15.7 %all-to-all-start = ((bf16[256,32,1024]{2,1,0:T(8,128)(2,1)}), bf16[256,32,1024]{2,1,0:T(8,128)(2,1)}, u32[]{:S(2)}, u32[]{:S(2)}) async-start(bf16[256,32,1024]{2,1,0:T(8,128)(2,1)} %stack.2), calls=%async_computation | async-start | bytes 33554432 | tf_op jit(solution)/shard_map/all_to_all | solution.py:104
  29.1 2.1 fusion.1
  31.1 8.2 %collective-permute-start = (bf16[24,24,1,128]{3,1,2,0:T(8,128)(2,1)S(1)}, bf16[24,24,1,128]{3,1,2,0:T(8,128)(2,1)S(1)}, u32[]{:S(2)}, u32[]{:S(2)}) collective-permute-start(bf16[24,24,1,128]{3,1,2,0:T(8,128)(2,1)S(1)} %get-tuple-element.9), channel_id=1, source_target_pairs={{0,1},{1,2},{2,3},{3,4},{4,5},{5,6},{6,7},{7,8},{8,9},{9,10},{10,1... | collective-permute-start | bytes 442376 | tf_op jit(solution)/shard_map/ppermute | solution.py:17
  39.4 4.5 collective-permute-start.1
  43.9 354.6 %collective-permute-done = bf16[24,24,1,128]{3,1,2,0:T(8,128)(2,1)S(1)} collective-permute-done((bf16[24,24,1,128]{3,1,2,0:T(8,128)(2,1)S(1)}, bf16[24,24,1,128]{3,1,2,0:T(8,128)(2,1)S(1)}, u32[]{:S(2)}, u32[]{:S(2)}) %collective-permute-start) | collective-permute-done | bytes 147488 | tf_op jit(solution)/shard_map/ppermute | solution.py:17
  398.6 6.9 %collective-permute-done.1 = bf16[24,24,1,128]{3,1,2,0:T(8,128)(2,1)S(1)} collective-permute-done((bf16[24,24,1,128]{3,1,2,0:T(8,128)(2,1)S(1)}, bf16[24,24,1,128]{3,1,2,0:T(8,128)(2,1)S(1)}, u32[]{:S(2)}, u32[]{:S(2)}) %collective-permute-start.1) | collective-permute-done | bytes 147488 | tf_op jit(solution)/shard_map/ppermute | solution.py:17
  405.6 0.3 pad_maximum_fusion.2
  405.8 3.4 collective-permute-start.2
  409.2 4.6 collective-permute-start.3
  413.8 2.1 collective-permute-done.2
  416.2 1.0 collective-permute-done.3
  417.4 0.8 pad_maximum_fusion.4
  418.1 2.0 collective-permute-start.5
  420.2 4.2 collective-permute-start.4
  424.4 0.6 collective-permute-done.5
  425.0 1.9 collective-permute-done.4
  426.9 1.9 fusion.4
  428.9 0.2 slice_dynamic-update-slice_fusion.25
  429.2 0.2 slice_dynamic-update-slice_fusion.24
  429.4 0.3 slice_dynamic-update-slice_fusion.23
  429.7 0.3 slice_dynamic-update-slice_fusion.22
  430.1 0.3 slice_dynamic-update-slice_fusion.21
  430.4 0.3 slice_dynamic-update-slice_fusion.20
  430.7 0.3 slice_dynamic-update-slice_fusion.19
  431.1 0.3 slice_dynamic-update-slice_fusion.18
  431.4 0.2 slice_dynamic-update-slice_fusion.17
  431.7 0.2 slice_dynamic-update-slice_fusion.16
  432.1 0.3 slice_dynamic-update-slice_fusion.14
  432.5 0.3 slice_dynamic-update-slice_fusion.13
  432.8 0.3 slice_dynamic-update-slice_fusion.12
  433.1 0.3 slice_dynamic-update-slice_fusion.11
  433.5 0.3 slice_dynamic-update-slice_fusion.10
  433.8 0.3 slice_dynamic-update-slice_fusion.9
  434.9 0.3 slice_dynamic-update-slice_fusion.5
  435.2 0.3 slice_dynamic-update-slice_fusion.4
  435.5 0.3 slice_dynamic-update-slice_fusion.3
  435.9 0.3 slice_dynamic-update-slice_fusion.2
  436.2 0.3 slice_dynamic-update-slice_fusion.1
  436.5 0.3 slice_dynamic-update-slice_fusion
  436.9 20.4 %copy.70 = bf16[12,12,12,3456]{3,2,1,0:T(8,128)(2,1)} copy(bf16[12,12,12,3456]{3,1,2,0:T(8,128)(2,1)S(1)} %slice_dynamic-update-slice_fusion) | data formatting | bytes 23887872 | tf_op jit(solution)/shard_map/concatenate | solution.py:42
  457.3 18.6 %reshape.97 = bf16[1728,3456]{1,0:T(8,128)(2,1)} reshape(bf16[12,12,12,3456]{3,2,1,0:T(8,128)(2,1)} %copy.70) | data formatting | bytes 23887872 | tf_op jit(solution)/shard_map/reshape | solution.py:51
  475.9 7.7 %multiply_convert_fusion = bf16[1728,128]{1,0:T(8,128)(2,1)S(1)} fusion(bf16[1728,3456]{1,0:T(8,128)(2,1)} %reshape.97, bf16[3456,128]{1,0:T(8,128)(2,1)S(1)} %bitcast.24, f32[128]{0:T(128)S(1)} %copy-done.5), kind=kOutput, calls=%fused_computation.14 | convolution fusion | flops 1530150912 | bytes 13271552 | tf_op jit(solution)/shard_map/dot_general | solution.py:52
  483.6 17.3 %copy.71 = bf16[3,4,3,4,3,4,128]{5,3,1,6,4,2,0:T(4,128)(2,1)} copy(bf16[3,4,3,4,3,4,128]{6,5,4,3,2,1,0:T(4,128)(2,1)S(1)} %bitcast.34) | data formatting | bytes 884736 | tf_op jit(solution)/shard_map/reshape;reshape | solution.py:60
  500.9 37.1 %reshape_stack_reshape.3 = bf16[27,8192]{1,0:T(8,128)(2,1)S(1)} reshape(bf16[3,3,3,128,4,4,4]{6,5,4,3,2,1,0:T(4,128)(2,1)} %bitcast.25) | data formatting | bytes 884736 | tf_op jit(solution)/shard_map/reshape;stack;reshape | solution.py:100
  538.0 8.8 %fusion.2 = bf16[27,1024]{1,0:T(8,128)(2,1)S(1)} fusion(bf16[27,8192]{1,0:T(8,128)(2,1)S(1)} %reshape_stack_reshape.3, bf16[8192,1024]{1,0:T(8,128)(2,1)} %bitcast.4, f32[1024]{0:T(1024)S(1)} %copy-done.2), kind=kOutput, calls=%fused_computation.13 | convolution fusion | flops 453040128 | bytes 17278976 | tf_op jit(solution)/shard_map/dot_general | solution.py:101
  546.8 9.0 %all_to_all.21 = bf16[27,8,128]{2,0,1:T(8,128)(2,1)S(1)} all-to-all(bf16[27,8,128]{2,0,1:T(8,128)(2,1)S(1)} %copy.72), channel_id=1, replica_groups=mesh['chan'=8,'region'=32] {'chan'}, dimensions={1} | all-to-all | bytes 110592 | tf_op jit(solution)/shard_map/all_to_all | solution.py:115
  556.0 4.2 collective-permute-start.6
  560.2 8.7 %collective-permute-start.7 = (bf16[2,6,6,1,128]{4,0,3,2,1:T(2,128)(2,1)S(1)}, bf16[2,6,6,1,128]{4,0,3,2,1:T(2,128)(2,1)S(1)}, u32[]{:S(2)}, u32[]{:S(2)}) collective-permute-start(bf16[2,6,6,1,128]{4,0,3,2,1:T(2,128)(2,1)S(1)} %get-tuple-element.48), channel_id=1, source_target_pairs={{1,0},{2,1},{3,2},{4,3},{5,4},{6,5},{7,6},{8,7},{9,8},{10,9},{11,1... | collective-permute-start | bytes 55304 | tf_op jit(solution)/shard_map/ppermute | solution.py:17
  569.1 1.4 collective-permute-done.7
  570.5 3.2 collective-permute-start.8
  573.9 4.8 collective-permute-start.9
  578.8 1.3 collective-permute-done.9
  580.1 0.3 pad_maximum_fusion.9
  580.5 3.6 collective-permute-start.10
  584.4 2.3 collective-permute-start.11
  587.1 2.9 collective-permute-done.11
  590.1 0.5 pad_maximum_fusion.3
  590.6 0.6 fusion.10
  593.3 5.8 fusion.16
  599.8 0.8 dynamic_slice.7
  600.5 36.9 %reduce-scatter.2.cloned.1.call-done = f32[216,128]{1,0:T(8,128)} async-done(((f32[216,1024]{1,0:T(8,128)}), f32[216,128]{1,0:T(8,128)}) %reduce-scatter.2.cloned.1.call-update) | async-done | bytes 110608 | tf_op jit(solution)/shard_map/reduce_scatter | solution.py:134
  637.4 0.9 divide_multiply_fusion
  638.5 0.6 add_convert_fusion
  (130 shorter events, 4.8 us)
Async XLA Ops:
  6.5 469.4 %copy-start = (bf16[3,3,3,128,128]{4,3,2,1,0:T(8,128)(2,1)S(1)}, bf16[3,3,3,128,128]{4,3,2,1,0:T(8,128)(2,1)}, u32[]{:S(2)}) copy-start(bf16[3,3,3,128,128]{4,3,2,1,0:T(8,128)(2,1)} %param.13) | copy-start | bytes 2654212
  13.3 15.8 %copy-start.3 = (f32[128]{0:T(128)S(1)}, f32[128]{0:T(128)}, u32[]{:S(2)}) copy-start(f32[128]{0:T(128)} %param.12) | copy-start | bytes 1540
  13.3 15.8 %copy-start.4 = (f32[128]{0:T(128)S(1)}, f32[128]{0:T(128)}, u32[]{:S(2)}) copy-start(f32[128]{0:T(128)} %param.11) | copy-start | bytes 1540
  13.3 524.7 %all-to-all-start = ((bf16[256,32,1024]{2,1,0:T(8,128)(2,1)}), bf16[256,32,1024]{2,1,0:T(8,128)(2,1)}, u32[]{:S(2)}, u32[]{:S(2)}) async-start(bf16[256,32,1024]{2,1,0:T(8,128)(2,1)} %stack.2), calls=%async_computation | async-start | bytes 33554432 | tf_op jit(solution)/shard_map/all_to_all | solution.py:104
  29.0 608.5 %reduce-scatter.2.cloned.1.call-start = ((), (), s32[]{:S(2)}) async-start(), calls=%async_computation.3 | async-start | bytes 995328 | tf_op jit(solution)/shard_map/reduce_scatter | solution.py:134
  31.1 367.4 %collective-permute-start = (bf16[24,24,1,128]{3,1,2,0:T(8,128)(2,1)S(1)}, bf16[24,24,1,128]{3,1,2,0:T(8,128)(2,1)S(1)}, u32[]{:S(2)}, u32[]{:S(2)}) collective-permute-start(bf16[24,24,1,128]{3,1,2,0:T(8,128)(2,1)S(1)} %get-tuple-element.9), channel_id=1, source_target_pairs={{0,1},{1,2},{2,3},{3,4},{4,5},{5,6},{6,7},{7,8},{8,9},{9,10},{10,1... | collective-permute-start | bytes 442376 | tf_op jit(solution)/shard_map/ppermute | solution.py:17
  39.4 366.2 %collective-permute-start.1 = (bf16[24,24,1,128]{3,1,2,0:T(8,128)(2,1)S(1)}, bf16[24,24,1,128]{3,1,2,0:T(8,128)(2,1)S(1)}, u32[]{:S(2)}, u32[]{:S(2)}) collective-permute-start(bf16[24,24,1,128]{3,1,2,0:T(8,128)(2,1)S(1)} %get-tuple-element.10), channel_id=1, source_target_pairs={{1,0},{2,1},{3,2},{4,3},{5,4},{6,5},{7,6},{8,7},{9,8},{10,9},{11,1... | collective-permute-start | bytes 442376 | tf_op jit(solution)/shard_map/ppermute | solution.py:17
  405.8 10.1 %collective-permute-start.2 = (bf16[24,1,14,128]{3,1,2,0:T(2,128)(2,1)S(1)}, bf16[24,1,14,128]{3,1,2,0:T(2,128)(2,1)S(1)}, u32[]{:S(2)}, u32[]{:S(2)}) collective-permute-start(bf16[24,1,14,128]{3,1,2,0:T(2,128)(2,1)S(1)} %get-tuple-element.7), channel_id=1, source_target_pairs={{0,2},{1,3},{2,4},{3,5},{4,6},{5,7},{6,8},{7,9},{8,10},{9,11},{10,... | collective-permute-start | bytes 258056 | tf_op jit(solution)/shard_map/ppermute | solution.py:17
  409.2 8.0 %collective-permute-start.3 = (bf16[24,1,14,128]{3,1,2,0:T(2,128)(2,1)S(1)}, bf16[24,1,14,128]{3,1,2,0:T(2,128)(2,1)S(1)}, u32[]{:S(2)}, u32[]{:S(2)}) collective-permute-start(bf16[24,1,14,128]{3,1,2,0:T(2,128)(2,1)S(1)} %get-tuple-element.8), channel_id=1, source_target_pairs={{2,0},{3,1},{4,2},{5,3},{6,4},{7,5},{8,6},{9,7},{10,8},{11,9},{12,... | collective-permute-start | bytes 258056 | tf_op jit(solution)/shard_map/ppermute | solution.py:17
  418.1 6.9 %collective-permute-start.5 = (bf16[1,26,14,128]{3,1,2,0:T(8,128)(2,1)}, bf16[1,26,14,128]{3,1,2,0:T(8,128)(2,1)S(1)}, u32[]{:S(2)}, u32[]{:S(2)}) collective-permute-start(bf16[1,26,14,128]{3,1,2,0:T(8,128)(2,1)} %get-tuple-element.5), channel_id=1, source_target_pairs={{8,0},{9,1},{10,2},{11,3},{12,4},{13,5},{14,6},{15,7},{16,8},{17,9... | collective-permute-start | bytes 279560 | tf_op jit(solution)/shard_map/ppermute | solution.py:17
  420.2 6.7 %collective-permute-start.4 = (bf16[1,26,14,128]{3,1,2,0:T(8,128)(2,1)S(1)}, bf16[1,26,14,128]{3,1,2,0:T(8,128)(2,1)S(1)}, u32[]{:S(2)}, u32[]{:S(2)}) collective-permute-start(bf16[1,26,14,128]{3,1,2,0:T(8,128)(2,1)S(1)} %get-tuple-element.6), channel_id=1, source_target_pairs={{0,8},{1,9},{2,10},{3,11},{4,12},{5,13},{6,14},{7,15},{8,16},{9,17... | collective-permute-start | bytes 279560 | tf_op jit(solution)/shard_map/ppermute | solution.py:17
  457.3 18.6 %copy-start.5 = (f32[128]{0:T(128)S(1)}, f32[128]{0:T(128)}, u32[]{:S(2)}) copy-start(f32[128]{0:T(128)} %param.14) | copy-start | bytes 1540
  500.9 37.1 %copy-start.2 = (f32[1024]{0:T(1024)S(1)}, f32[1024]{0:T(1024)}, u32[]{:S(2)}) copy-start(f32[1024]{0:T(1024)} %param.16) | copy-start | bytes 12292
  556.0 13.0 %collective-permute-start.6 = (bf16[2,6,6,1,128]{4,0,3,2,1:T(2,128)(2,1)S(1)}, bf16[2,6,6,1,128]{4,0,3,2,1:T(2,128)(2,1)S(1)}, u32[]{:S(2)}, u32[]{:S(2)}) collective-permute-start(bf16[2,6,6,1,128]{4,0,3,2,1:T(2,128)(2,1)S(1)} %get-tuple-element.47), channel_id=1, source_target_pairs={{0,1},{1,2},{2,3},{3,4},{4,5},{5,6},{6,7},{7,8},{8,9},{9,10},{10,1... | collective-permute-start | bytes 55304 | tf_op jit(solution)/shard_map/ppermute | solution.py:17
  560.2 10.2 %collective-permute-start.7 = (bf16[2,6,6,1,128]{4,0,3,2,1:T(2,128)(2,1)S(1)}, bf16[2,6,6,1,128]{4,0,3,2,1:T(2,128)(2,1)S(1)}, u32[]{:S(2)}, u32[]{:S(2)}) collective-permute-start(bf16[2,6,6,1,128]{4,0,3,2,1:T(2,128)(2,1)S(1)} %get-tuple-element.48), channel_id=1, source_target_pairs={{1,0},{2,1},{3,2},{4,3},{5,4},{6,5},{7,6},{8,7},{9,8},{10,9},{11,1... | collective-permute-start | bytes 55304 | tf_op jit(solution)/shard_map/ppermute | solution.py:17
  570.5 8.3 %collective-permute-start.8 = (bf16[2,6,1,5,128]{4,0,3,2,1:T(2,128)(2,1)S(1)}, bf16[2,6,1,5,128]{4,0,3,2,1:T(2,128)(2,1)S(1)}, u32[]{:S(2)}, u32[]{:S(2)}) collective-permute-start(bf16[2,6,1,5,128]{4,0,3,2,1:T(2,128)(2,1)S(1)} %get-tuple-element.43), channel_id=1, source_target_pairs={{0,2},{1,3},{2,4},{3,5},{4,6},{5,7},{6,8},{7,9},{8,10},{9,11},{10,... | collective-permute-start | bytes 46088 | tf_op jit(solution)/shard_map/ppermute | solution.py:17
  573.9 6.2 collective-permute-start.9
  580.5 6.6 %collective-permute-start.10 = (bf16[2,1,8,5,128]{4,0,3,2,1:T(2,128)(2,1)S(1)}, bf16[2,1,8,5,128]{4,0,3,2,1:T(2,128)(2,1)S(1)}, u32[]{:S(2)}, u32[]{:S(2)}) collective-permute-start(bf16[2,1,8,5,128]{4,0,3,2,1:T(2,128)(2,1)S(1)} %get-tuple-element.32), channel_id=1, source_target_pairs={{0,8},{1,9},{2,10},{3,11},{4,12},{5,13},{6,14},{7,15},{8,16},{9,17... | collective-permute-start | bytes 61448 | tf_op jit(solution)/shard_map/ppermute | solution.py:17
  584.4 5.7 collective-permute-start.11
  593.3 45.8 %copy-start.1 = (bf16[3,3,3,128,128]{4,3,2,1,0:T(8,128)(2,1)S(1)}, bf16[3,3,3,128,128]{4,3,2,1,0:T(8,128)(2,1)}, u32[]{:S(2)}) copy-start(bf16[3,3,3,128,128]{4,3,2,1,0:T(8,128)(2,1)} %param.13) | copy-start | bytes 2654212
Sparse Core Ops, SparseCore 0:
  599.2 38.1 reduce-scatter.1
